TPU v7x, 32 devices: a whole 2x2x4 slice. The times are simulated.
32 devices in a mesh: groups: 2 (over y), seq: 4 (over z), dp: 4 (over x, core).
Axes of the slice: x: 2, y: 2, z: 4, core: 2. Of those that a mesh axis runs over, the one named last changes fastest.
Arguments:
- scan_input: bfloat16 [8, 512, 2048], P(('groups', 'dp'), 'seq'), parts along dimension 0, may hold values from -6 to 6
- gate_input: bfloat16 [8, 512, 2048], P(('groups', 'dp'), 'seq'), parts along dimension 0, may hold values from -6 to 6
- bmat: bfloat16 [8, 512, 128], P(('groups', 'dp'), 'seq'), parts along dimension 0, may hold values from -6 to 6
- cmat: bfloat16 [8, 512, 128], P(('groups', 'dp'), 'seq'), parts along dimension 0, may hold values from -0.5 to 0.5
- dt_raw: float32 [8, 512, 64], P(('groups', 'dp'), 'seq'), parts along dimension 0, may hold values from -4 to 4
- a_log: float32 [64], replicated
- d_skip: float32 [64], replicated, may hold values from 0.5 to 1.5
- gain: float32 [2048], replicated, may hold values from 0.1 to 1.9
- spans: int32 [8, 8, 2], P(('groups', 'dp')), parts along dimension 0, may hold values from 0 to 512, as said below
- cot: bfloat16 [8, 512, 2048], P(('groups', 'dp'), 'seq'), parts along dimension 0, may hold values from -6 to 6
Outputs:
- grad_x: bfloat16 [8, 512, 2048], P(('groups', 'dp'), 'seq'), parts along dimension 0
- grad_b: bfloat16 [8, 512, 128], P(('groups', 'dp'), 'seq'), parts along dimension 0
- grad_c: bfloat16 [8, 512, 128], P(('groups', 'dp'), 'seq'), parts along dimension 0
- grad_dt: float32 [8, 512, 64], P(('groups', 'dp'), 'seq'), parts along dimension 0
- grad_alog: float32 [128], P('groups'), parts along dimension 0
- grad_skip: float32 [128], P('groups'), parts along dimension 0
- grad_gain: float32 [4096], P('groups'), parts along dimension 0
There are 2 independent parts, one for each index of `groups`. A program takes and returns all parts, laid end to end along the dimension named above; an argument that names none is the same for every part. Nothing has to cross between parts.
Inputs may be any that keep to these rules, and one draw needn't show every extreme that they name: For each sequence the 8 spans are in order and tile the positions: the first starts at 0, each ends (exclusive) where the next starts, the last ends at 512, none is empty.
All inputs are finite; a program needn't handle non-finite values.
Results may differ from a plain program's by a relative error of at most 0.001.
Values sent between devices are 32-bit elements; how exact they have to be, the bound alone decides.
A program may use at most 128 MiB of HBM per device.

v0:
```python
import jax
import jax.numpy as jnp
from jax import lax
from jax.sharding import PartitionSpec as P

EPS = 1e-05
HI = lax.Precision.HIGHEST


def entering(shard, axis, combine, identity, reverse):
    peers, position = (lax.axis_size(axis), lax.axis_index(axis))
    everything = jax.tree.map(lambda part: lax.all_gather(part, axis), shard)
    start = jax.tree.map(
        lambda part, zero: jnp.broadcast_to(jnp.asarray(zero, part.dtype), part.shape),
        shard,
        identity,
    )

    def step(k, before):
        at = peers - 1 - k if reverse else k
        reached = at > position if reverse else at < position
        new = combine(before, jax.tree.map(lambda part: part[at], everything))
        return jax.tree.map(lambda a, b: jnp.where(reached, a, b), new, before)

    return lax.fori_loop(0, peers, step, start)


def combine(earlier, later):
    return (earlier[0] * later[0], later[0][:, None, None] * earlier[1] + later[1])


def on_device(scan_input, gate_input, bmat, cmat, dt_raw, a_log, d_skip, gain, spans, cot):
    rows = scan_input.shape[1]
    width = scan_input.shape[2]
    heads = a_log.shape[0]
    hdim = width // heads
    offset = lax.axis_index("seq") * rows
    xs = scan_input[0].astype(jnp.float32).reshape(rows, heads, hdim)
    zs = gate_input[0].astype(jnp.float32)
    bs = bmat[0].astype(jnp.float32)
    cs = cmat[0].astype(jnp.float32)
    raw = dt_raw[0]
    where_at = offset + jnp.arange(rows)
    flags = jnp.any(where_at[:, None] == spans[0][None, :, 0], 1).astype(jnp.int32)
    segl = jnp.cumsum(flags)
    step_size = jax.nn.softplus(raw)
    rate = jnp.exp(a_log)
    la = -rate[None, :] * step_size
    cum = jnp.cumsum(la, 0)
    place = jnp.arange(rows)
    same = (place[:, None] >= place[None, :]) & (segl[:, None] == segl[None, :])
    lmat = jnp.exp(jnp.where(same[None], cum.T[:, :, None] - cum.T[:, None, :], -jnp.inf))
    gmat = jnp.dot(cs, bs.T, precision=HI)
    xdt = xs * step_size[:, :, None]
    win = jnp.where((segl == 0)[:, None], jnp.exp(cum), 0.0)
    wout = jnp.exp(jnp.where((segl == segl[-1])[:, None], cum[-1][None, :] - cum, -jnp.inf))
    ablk = jnp.where(segl[-1] == 0, jnp.exp(cum[-1]), 0.0)
    weighted = xdt * wout[:, :, None]
    hloc = jnp.einsum("jhp,jn->hpn", weighted, bs, precision=HI)
    empty = jnp.zeros_like(hloc)
    _, hin = entering((ablk, hloc), "seq", combine, (jnp.ones_like(ablk), empty), False)
    sweights = lmat * gmat[None]
    y_intra = jnp.einsum("hij,jhp->ihp", sweights, xdt, precision=HI)
    cproj = jnp.einsum("in,hpn->ihp", cs, hin, precision=HI)
    y = y_intra + win[:, :, None] * cproj + d_skip[None, :, None] * xs
    gate = jax.nn.silu(zs)
    gated = y.reshape(rows, width) * gate
    scale = lax.rsqrt(jnp.mean(gated * gated, 1, keepdims=True) + EPS)
    normed = gated * scale
    upstream = cot[0].astype(jnp.float32)
    part_gain = jnp.sum(upstream * normed, 0)
    dnorm = upstream * gain[None, :]
    dgated = scale * dnorm - normed * scale * jnp.mean(dnorm * normed, 1, keepdims=True)
    dy = (dgated * gate).reshape(rows, heads, hdim)
    part_skip = jnp.sum(dy * xs, (0, 2))
    grad_in = dy * d_skip[None, :, None]
    dxdt = jnp.einsum("hij,ihp->jhp", sweights, dy, precision=HI)
    dsw = jnp.einsum("ihp,jhp->hij", dy, xdt, precision=HI)
    dgm = jnp.sum(dsw * lmat, 0)
    qmat = dsw * sweights
    dcum = jnp.sum(qmat, 2).T - jnp.sum(qmat, 1).T
    grad_c = jnp.dot(dgm, bs, precision=HI)
    grad_b = jnp.dot(dgm.T, cs, precision=HI)
    dwin = jnp.sum(dy * cproj, 2)
    dcum = dcum + dwin * win
    wdy = dy * win[:, :, None]
    grad_c = grad_c + jnp.einsum("ihp,hpn->in", wdy, hin, precision=HI)
    dhin = jnp.einsum("ihp,in->hpn", wdy, cs, precision=HI)
    _, gend = entering((ablk, dhin), "seq", combine, (jnp.ones_like(ablk), empty), True)
    vproj = jnp.einsum("jn,hpn->jhp", bs, gend, precision=HI)
    dwout = jnp.sum(vproj * xdt, 2)
    dxdt = dxdt + vproj * wout[:, :, None]
    grad_b = grad_b + jnp.einsum("jhp,hpn->jn", weighted, gend, precision=HI)
    tail = dwout * wout
    dablk = jnp.sum(gend * hin, (1, 2))
    lastrow = (place == rows - 1)[:, None]
    dcum = dcum - tail + jnp.where(lastrow, (jnp.sum(tail, 0) + dablk * ablk)[None, :], 0.0)
    grad_in = grad_in + dxdt * step_size[:, :, None]
    dstep = jnp.sum(dxdt * xs, 2)
    dla = jnp.flip(jnp.cumsum(jnp.flip(dcum, 0), 0), 0)
    dstep = dstep - rate[None, :] * dla
    part_alog = jnp.sum(dla * la, 0)
    grad_dt = dstep * jax.nn.sigmoid(raw)
    grad_alog, grad_skip, grad_gain = lax.psum((part_alog, part_skip, part_gain), ("seq", "dp"))
    return (
        grad_in.reshape(rows, width).astype(jnp.bfloat16)[None],
        grad_b.astype(jnp.bfloat16)[None],
        grad_c.astype(jnp.bfloat16)[None],
        grad_dt[None],
        grad_alog,
        grad_skip,
        grad_gain,
    )


def solution(mesh):
    return jax.shard_map(
        on_device,
        mesh=mesh,
        in_specs=(
            P(("groups", "dp"), "seq", None),
            P(("groups", "dp"), "seq", None),
            P(("groups", "dp"), "seq", None),
            P(("groups", "dp"), "seq", None),
            P(("groups", "dp"), "seq", None),
            P(),
            P(),
            P(),
            P(("groups", "dp"), None, None),
            P(("groups", "dp"), "seq", None),
        ),
        out_specs=(
            P(("groups", "dp"), "seq", None),
            P(("groups", "dp"), "seq", None),
            P(("groups", "dp"), "seq", None),
            P(("groups", "dp"), "seq", None),
            P("groups"),
            P("groups"),
            P("groups"),
        ),
        check_vma=False,
    )
```

profile of v0, /device:TPU:0, one launch (start us, length us, event | category | flops | bytes accessed | tf_op | source)
XLA Modules:
  0.0 258.3 jit_solution(2906881014786928078)
XLA Ops:
  7.2 0.0 all-gather.6.cloned.1.call-start
  7.3 0.7 slice_bitcast_fusion
  8.0 0.1 compare_reduce_fusion
  8.1 0.1 copy.91
  8.2 0.2 broadcast_in_dim.97
  8.4 0.5 slice.15
  8.9 0.1 reduce.1
  9.0 1.2 fusion.89
  10.2 0.8 compare_select_fusion
  11.0 0.1 copy.92
  11.8 0.2 reduce_window_sum.24
  11.9 0.1 copy.95
  12.0 0.7 broadcast_compare_fusion.1
  12.7 1.3 copy.90
  14.0 0.1 exponential_select_fusion
  14.1 0.1 bitcast_multiply_fusion.3
  14.3 1.6 fusion.68
  15.8 0.0 all-gather.6.cloned.1.call-update
  15.9 0.0 all-gather.8.cloned.1.call-start
  15.9 0.7 copy.93
  16.6 1.2 copy.97
  17.9 1.2 copy.98
  19.1 0.1 mul.290
  19.2 12.6 %all-gather.2 = f32[4,1,64]{2,1,0:T(1,128)S(1)} all-gather(f32[1,1,64]{2,1,0:T(1,128)S(1)} %get-tuple-element.340), channel_id=1, replica_groups=mesh['groups'=2,'seq'=4,'dp'=4] {'seq'}, dimensions={0}, use_global_device_ids=true | all-gather | bytes 1280 | tf_op jit(solution)/shard_map/all_gather | solution.py:12
  31.8 0.1 fusion.62
  31.9 0.1 fusion.71
  32.1 67.4 %all-gather.6.cloned.1.call-done = f32[256,32,128]{2,1,0:T(8,128)} async-done(((f32[64,32,128]{2,1,0:T(8,128)}), f32[256,32,128]{2,1,0:T(8,128)}) %all-gather.6.cloned.1.call-update) | async-done | bytes 4194320 | tf_op jit(solution)/shard_map/all_gather | solution.py:12
  99.5 6.1 %while.30 = (s32[]{:T(128)}, f32[64,32,128]{2,1,0:T(8,128)S(1)}, s32[]{:T(128)}, f32[4,64]{1,0:T(4,128)S(1)}, f32[4,64,32,128]{3,2,1,0:T(8,128)}, /*index=5*/s32[]{:T(128)}, s32[]{:T(128)}) while((s32[]{:T(128)}, f32[64,32,128]{2,1,0:T(8,128)S(1)}, s32[]{:T(128)}, f32[4,64]{1,0:T(4,128)S(1)}, f32[4,64,32,128]{3,2,1,0:T(8,128)}, ...), condition=%wide.region_4.5_spmd.clone, body=%wide.region_3.4_spmd.clone.sunk | while | flops 1048580 | bytes 3146601 | solution.py:25
  99.5 1.5 fusion.104
  101.0 1.5 fusion.104
  102.6 1.5 fusion.104
  104.1 1.5 fusion.104
  105.6 0.6 convolution_bitcast_fusion.1
  106.2 8.4 %multiply_reduce_fusion.6 = (f32[128]{0:T(128)S(1)}, f32[128,64,32]{0,2,1:T(8,128)S(1)}) fusion(f32[128,64,32]{0,2,1:T(8,128)S(1)} %bitcast.171, f32[64]{0:T(128)S(1)} %copy-done.17, f32[128,64,32]{0,2,1:T(8,128)S(1)} %convolution_bitcast_fusion.1, f32[128,64]{0,1:T(8,128)S(1)} %get-tuple-element.343, f32[128,128]{1,0:T(8,128)S(1)} %fusion.71, ...), kind=kOutput, calls=%fused_computation.61 | convolution fusion | flops 409468800 | bytes 3851008 | tf_op jit(solution)/shard_map/hij,jhp->ihp/dot_general | solution.py:63
  114.6 1.4 copy.99
  116.0 2.2 fusion.46
  118.2 2.1 subtract_multiply_fusion
  120.3 1.6 fusion.49
  121.9 0.0 all-gather.8.cloned.1.call-update
  122.0 0.5 iota_compare_fusion.1
  122.5 1.8 convolution_bitcast_fusion.2
  124.3 10.8 %fusion.8 = (f32[64,128]{1,0:T(8,128)}, f32[64,128]{1,0:T(8,128)}, f32[128,128]{1,0:T(8,128)S(1)}) fusion(f32[128,128]{1,0:T(8,128)S(1)} %fusion.71, f32[64,128]{1,0:T(8,128)} %copy.93, pred[128,128]{1,0:T(8,128)(4,1)} %copy-done.13, f32[128,64,32]{0,2,1:T(8,128)S(1)} %subtract_multiply_fusion, f32[128,64]{0,1:T(8,128)S(1)} %get-tuple-element.345, ...), kind=kOutput, calls=%fused_computation.12 | convolution fusion | flops 411533312 | bytes 1851392 | tf_op jit(solution)/shard_map/ihp,jhp->hij/dot_general | solution.py:78
  135.2 0.8 fusion.37
  136.0 65.4 %all-gather.8.cloned.1.call-done = f32[256,32,128]{2,1,0:T(8,128)} async-done(((f32[64,32,128]{2,1,0:T(8,128)}), f32[256,32,128]{2,1,0:T(8,128)}) %all-gather.8.cloned.1.call-update) | async-done | bytes 4194320 | tf_op jit(solution)/shard_map/all_gather | solution.py:12
  201.4 6.1 %while.31 = (s32[]{:T(128)}, f32[64,32,128]{2,1,0:T(8,128)S(1)}, s32[]{:T(128)}, f32[4,64]{1,0:T(4,128)S(1)}, f32[4,64,32,128]{3,2,1,0:T(8,128)}, /*index=5*/s32[]{:T(128)}, s32[]{:T(128)}, s32[]{:T(128)}, s32[]{:T(128)}) while((s32[]{:T(128)}, f32[64,32,128]{2,1,0:T(8,128)S(1)}, s32[]{:T(128)}, f32[4,64]{1,0:T(4,128)S(1)}, ...), condition=%wide.region_8.9_spmd.clone, body=%wide.region_7.8_spmd.clone.sunk | while | flops 1048584 | bytes 3146663 | solution.py:25
  201.4 1.5 fusion.105
  202.9 1.5 fusion.105
  204.5 1.5 fusion.105
  206.0 1.5 fusion.105
  207.6 0.6 convolution_bitcast_fusion
  208.2 0.6 multiply_reduce_fusion.2
  208.8 1.9 convolution_bitcast_fusion.3
  210.7 4.9 %multiply_reduce_fusion.1 = (f32[64]{0:T(128)S(1)}, f32[128,64]{0,1:T(8,128)S(1)}, f32[128,64]{0,1:T(8,128)S(1)}, f32[128,64]{0,1:T(8,128)S(1)}, bf16[128,64,32]{0,2,1:T(8,128)(2,1)S(1)}) fusion(f32[128,64,32]{0,2,1:T(8,128)S(1)} %subtract_multiply_fusion, f32[128,64,32]{0,2,1:T(8,128)S(1)} %convolution_bitcast_fusion, ...), kind=kOutput, calls=%fused_computation.53 | convolution fusion | flops 409968576 | bytes 4473344 | tf_op jit(solution)/shard_map/hij,ihp->jhp/dot_general | solution.py:77
  215.6 0.1 multiply_reduce_fusion.8
  215.7 0.1 fusion.64
  215.8 0.1 rev.7
  215.9 0.1 copy.100
  216.0 0.2 reduce_window_sum.25
  216.2 0.1 copy.101
  216.2 0.1 rev.8
  216.3 0.9 fusion.38
  217.2 1.0 copy.102
  218.2 0.8 multiply_reduce_fusion.7
  219.0 32.4 %all-reduce = (f32[64]{0:T(128)}, f32[64]{0:T(128)}, f32[2048]{0:T(1024)}) all-reduce(f32[64]{0:T(128)S(1)} %get-tuple-element.341, f32[64]{0:T(128)S(1)} %get-tuple-element.311, f32[2048]{0:T(1024)S(1)} %get-tuple-element.309), channel_id=1, replica_groups=mesh['groups'=2,'seq'=4,'dp'=4] {'seq','dp'}, use_global_device_ids=true, to_apply=%region_19.20 | all-reduce | flops 2176 | bytes 17408 | tf_op jit(solution)/shard_map/psum | solution.py:104
  (54 shorter events, 0.2 us)
Async XLA Ops:
  7.2 7.1 %copy-start = (bf16[1,128,128]{2,1,0:T(8,128)(2,1)S(1)}, bf16[1,128,128]{2,1,0:T(8,128)(2,1)}, u32[]{:S(2)}) copy-start(bf16[1,128,128]{2,1,0:T(8,128)(2,1)} %param.16) | copy-start | bytes 98308
  7.2 10.7 %copy-start.4 = (bf16[1,128,2048]{2,1,0:T(8,128)(2,1)S(1)}, bf16[1,128,2048]{2,1,0:T(8,128)(2,1)}, u32[]{:S(2)}) copy-start(bf16[1,128,2048]{2,1,0:T(8,128)(2,1)} %param.23) | copy-start | bytes 1572868
  7.2 92.3 %all-gather.6.cloned.1.call-start = ((), (), s32[]{:S(2)}) async-start(), calls=%async_computation | async-start | bytes 5242880 | tf_op jit(solution)/shard_map/all_gather | solution.py:12
  14.0 85.5 %copy-start.2 = (bf16[1,128,2048]{1,2,0:T(8,128)(2,1)}, bf16[1,128,2048]{1,2,0:T(8,128)(2,1)S(1)}, u32[]{:S(2)}) copy-start(bf16[1,128,2048]{1,2,0:T(8,128)(2,1)S(1)} %copy.90) | copy-start | bytes 1572868
  14.0 5.1 %copy-start.9 = (f32[2048]{0:T(1024)S(1)}, f32[2048]{0:T(1024)}, u32[]{:S(2)}) copy-start(f32[2048]{0:T(1024)} %param.21) | copy-start | bytes 24580
  14.0 17.9 %copy-start.7 = (bf16[1,128,128]{2,1,0:T(8,128)(2,1)S(1)}, bf16[1,128,128]{2,1,0:T(8,128)(2,1)}, u32[]{:S(2)}) copy-start(bf16[1,128,128]{2,1,0:T(8,128)(2,1)} %param.17) | copy-start | bytes 98308
  15.9 185.5 %all-gather.8.cloned.1.call-start = ((), (), s32[]{:S(2)}) async-start(), calls=%async_computation.1 | async-start | bytes 5242880 | tf_op jit(solution)/shard_map/all_gather | solution.py:12
  31.9 74.3 %copy-start.13 = (pred[128,128]{1,0:T(8,128)(4,1)}, pred[128,128]{1,0:T(8,128)(4,1)S(1)}, u32[]{:S(2)}) copy-start(pred[128,128]{1,0:T(8,128)(4,1)S(1)} %fusion.62) | copy-start | bytes 49156
  99.5 6.7 %copy-start.17 = (f32[64]{0:T(128)S(1)}, f32[64]{0:T(128)}, u32[]{:S(2)}) copy-start(f32[64]{0:T(128)} %param.20) | copy-start | bytes 772
  106.2 8.4 %copy-start.5 = (f32[128,64,32]{0,2,1:T(8,128)}, f32[128,64,32]{0,2,1:T(8,128)S(1)}, u32[]{:S(2)}) copy-start(f32[128,64,32]{0,2,1:T(8,128)S(1)} %convolution_bitcast_fusion.1) | copy-start | bytes 3145732
  114.6 3.6 %copy-start.1 = (f32[128,64,32]{0,2,1:T(8,128)}, f32[128,64,32]{0,2,1:T(8,128)S(1)}, u32[]{:S(2)}) copy-start(f32[128,64,32]{0,2,1:T(8,128)S(1)} %get-tuple-element.352) | copy-start | bytes 3145732
  207.5 1.2 copy-start.3
  207.5 3.1 %copy-start.6 = (f32[128,64,32]{0,2,1:T(8,128)S(1)}, f32[128,64,32]{0,2,1:T(8,128)}, u32[]{:S(2)}) copy-start(f32[128,64,32]{0,2,1:T(8,128)} %copy-done.5) | copy-start | bytes 3145732
  207.5 3.1 %copy-start.10 = (f32[64,128]{1,0:T(8,128)S(1)}, f32[64,128]{1,0:T(8,128)}, u32[]{:S(2)}) copy-start(f32[64,128]{1,0:T(8,128)} %copy.93) | copy-start | bytes 98308
  207.6 3.1 %copy-start.14 = (pred[128,128]{1,0:T(8,128)(4,1)S(1)}, pred[128,128]{1,0:T(8,128)(4,1)}, u32[]{:S(2)}) copy-start(pred[128,128]{1,0:T(8,128)(4,1)} %copy-done.13) | copy-start | bytes 49156
  207.6 3.1 %copy-start.18 = (f32[64]{0:T(128)S(1)}, f32[64]{0:T(128)}, u32[]{:S(2)}) copy-start(f32[64]{0:T(128)} %param.20) | copy-start | bytes 772
  210.7 5.0 %copy-start.11 = (f32[64,128]{1,0:T(8,128)S(1)}, f32[64,128]{1,0:T(8,128)}, u32[]{:S(2)}) copy-start(f32[64,128]{1,0:T(8,128)} %get-tuple-element.306) | copy-start | bytes 98308
  210.7 5.0 %copy-start.12 = (f32[64,128]{1,0:T(8,128)S(1)}, f32[64,128]{1,0:T(8,128)}, u32[]{:S(2)}) copy-start(f32[64,128]{1,0:T(8,128)} %get-tuple-element.307) | copy-start | bytes 98308
  210.7 5.0 %copy-start.16 = (pred[128]{0:T(512)(128)(4,1)S(1)}, pred[128]{0:T(512)(128)(4,1)}, u32[]{:S(2)}) copy-start(pred[128]{0:T(512)(128)(4,1)} %iota_compare_fusion.1) | copy-start | bytes 388
  210.7 7.5 %copy-start.8 = (f32[1,128,64]{1,2,0:T(8,128)S(1)}, f32[1,128,64]{1,2,0:T(8,128)}, u32[]{:S(2)}) copy-start(f32[1,128,64]{1,2,0:T(8,128)} %param.18) | copy-start | bytes 98308
  210.7 7.5 %copy-start.15 = (f32[64]{0:T(128)S(1)}, f32[64]{0:T(128)}, u32[]{:S(2)}) copy-start(f32[64]{0:T(128)} %get-tuple-element.347) | copy-start | bytes 772
Sparse Core Ops, SparseCore 0:
  16.0 83.4 all-gather.5
  122.1 79.2 all-gather.7
where the time goes:
time: 259 us; the launch traced here: 258 us
  waiting for transfers between devices  133 us (51%)
  blocking collectives  45.1 us (17%)
  matrix products  34 us (13%)
  other arithmetic  21.9 us (8%)
  between operations  15.1 us (6%)
  local copies, waits for them, and re-layouts  8.92 us (3%)
    all_gather x2, waiting for transfers between devices, entering(): everything = jax.tree.map(lambda part: lax.all_gather(part, axis), shard)  133 us
    psum x1, blocking collectives, on_device(): lax.psum((part_alog, part_skip, part_gain), ('seq', 'dp'))  32.4 us
    all_gather x1, blocking collectives, entering(): everything = jax.tree.map(lambda part: lax.all_gather(part, axis), shard)  12.6 us
    select_n x8, other arithmetic, step(): return jax.tree.map(lambda a, b: jnp.where(reached, a, b), new, before)  11.9 us
    dot_general x1, matrix products, on_device(): dsw = jnp.einsum('ihp,jhp->hij', dy, xdt, precision=HI)  10.8 us
    dot_general x1, matrix products, on_device(): y_intra = jnp.einsum('hij,jhp->ihp', sweights, xdt, precision=HI)  8.38 us
  transfers between devices with their start and end apart: 2, of which 2 were waited for; matrix products, arithmetic and copies ran while one was open for 7% of the time, Pallas kernels for 0%

commit v1 on v0

--- a/solution.py
+++ b/solution.py
@@ -101,7 +101,9 @@
     dstep = dstep - rate[None, :] * dla
     part_alog = jnp.sum(dla * la, 0)
     grad_dt = dstep * jax.nn.sigmoid(raw)
-    grad_alog, grad_skip, grad_gain = lax.psum((part_alog, part_skip, part_gain), ("seq", "dp"))
+    grad_alog, grad_skip, grad_gain = lax.psum(
+        lax.psum((part_alog, part_skip, part_gain), "dp"), "seq"
+    )
     return (
         grad_in.reshape(rows, width).astype(jnp.bfloat16)[None],
         grad_b.astype(jnp.bfloat16)[None],

time: 259 us -> 244 us (0.942)
  blocking collectives: 45.1 us -> 29.8 us
    psum x1 -> x2, blocking collectives: 32.4 us -> 17.2 us  [the longest x1 9.96 us: on_device(): lax.psum(lax.psum((part_alog, part_skip, part_gain), 'dp'), 'seq')]
where the time goes in v1:
time: 244 us; the launch traced here: 243 us
  waiting for transfers between devices  133 us (55%)
  matrix products  34 us (14%)
  blocking collectives  29.8 us (12%)
  other arithmetic  21.9 us (9%)
  between operations  15.1 us (6%)
  local copies, waits for them, and re-layouts  8.92 us (4%)
    all_gather x2, waiting for transfers between devices, entering(): everything = jax.tree.map(lambda part: lax.all_gather(part, axis), shard)  133 us
    all_gather x1, blocking collectives, entering(): everything = jax.tree.map(lambda part: lax.all_gather(part, axis), shard)  12.6 us
    select_n x8, other arithmetic, step(): return jax.tree.map(lambda a, b: jnp.where(reached, a, b), new, before)  11.9 us
    dot_general x1, matrix products, on_device(): dsw = jnp.einsum('ihp,jhp->hij', dy, xdt, precision=HI)  10.8 us
    psum x1, blocking collectives, on_device(): lax.psum(lax.psum((part_alog, part_skip, part_gain), 'dp'), 'seq')  9.96 us
    dot_general x1, matrix products, on_device(): y_intra = jnp.einsum('hij,jhp->ihp', sweights, xdt, precision=HI)  8.38 us
    psum x1, blocking collectives, on_device(): lax.psum((part_alog, part_skip, part_gain), 'dp')  7.22 us
  transfers between devices with their start and end apart: 2, of which 2 were waited for; matrix products, arithmetic and copies ran while one was open for 7% of the time, Pallas kernels for 0%

profile of v1, /device:TPU:0, one launch (start us, length us, event | category | flops | bytes accessed | tf_op | source)
XLA Modules:
  0.0 243.0 jit_solution(13497310739363138715)
XLA Ops:
  7.2 0.0 all-gather.6.cloned.1.call-start
  7.3 0.7 slice_bitcast_fusion
  8.0 0.1 compare_reduce_fusion
  8.1 0.1 copy.91
  8.2 0.2 broadcast_in_dim.97
  8.4 0.5 slice.15
  8.9 0.1 reduce.1
  9.0 1.2 fusion.89
  10.2 0.8 compare_select_fusion
  11.0 0.1 copy.92
  11.8 0.2 reduce_window_sum.24
  11.9 0.1 copy.95
  12.0 0.7 broadcast_compare_fusion.1
  12.7 1.3 copy.90
  14.0 0.1 exponential_select_fusion
  14.1 0.1 bitcast_multiply_fusion.3
  14.3 1.6 fusion.68
  15.8 0.0 all-gather.6.cloned.1.call-update
  15.9 0.0 all-gather.8.cloned.1.call-start
  15.9 0.7 copy.93
  16.6 1.2 copy.97
  17.9 1.2 copy.98
  19.1 0.1 mul.290
  19.2 12.6 %all-gather.2 = f32[4,1,64]{2,1,0:T(1,128)S(1)} all-gather(f32[1,1,64]{2,1,0:T(1,128)S(1)} %get-tuple-element.343), channel_id=1, replica_groups=mesh['groups'=2,'seq'=4,'dp'=4] {'seq'}, dimensions={0}, use_global_device_ids=true | all-gather | bytes 1280 | tf_op jit(solution)/shard_map/all_gather | solution.py:12
  31.8 0.1 fusion.62
  31.9 0.1 fusion.71
  32.1 67.4 %all-gather.6.cloned.1.call-done = f32[256,32,128]{2,1,0:T(8,128)} async-done(((f32[64,32,128]{2,1,0:T(8,128)}), f32[256,32,128]{2,1,0:T(8,128)}) %all-gather.6.cloned.1.call-update) | async-done | bytes 4194320 | tf_op jit(solution)/shard_map/all_gather | solution.py:12
  99.5 6.1 %while.30 = (s32[]{:T(128)}, f32[64,32,128]{2,1,0:T(8,128)S(1)}, s32[]{:T(128)}, f32[4,64]{1,0:T(4,128)S(1)}, f32[4,64,32,128]{3,2,1,0:T(8,128)}, /*index=5*/s32[]{:T(128)}, s32[]{:T(128)}) while((s32[]{:T(128)}, f32[64,32,128]{2,1,0:T(8,128)S(1)}, s32[]{:T(128)}, f32[4,64]{1,0:T(4,128)S(1)}, f32[4,64,32,128]{3,2,1,0:T(8,128)}, ...), condition=%wide.region_4.5_spmd.clone, body=%wide.region_3.4_spmd.clone.sunk | while | flops 1048580 | bytes 3146601 | solution.py:25
  99.5 1.5 fusion.104
  101.0 1.5 fusion.104
  102.6 1.5 fusion.104
  104.1 1.5 fusion.104
  105.6 0.6 convolution_bitcast_fusion.1
  106.2 8.4 %multiply_reduce_fusion.6 = (f32[128]{0:T(128)S(1)}, f32[128,64,32]{0,2,1:T(8,128)S(1)}) fusion(f32[128,64,32]{0,2,1:T(8,128)S(1)} %bitcast.171, f32[64]{0:T(128)S(1)} %copy-done.17, f32[128,64,32]{0,2,1:T(8,128)S(1)} %convolution_bitcast_fusion.1, f32[128,64]{0,1:T(8,128)S(1)} %get-tuple-element.346, f32[128,128]{1,0:T(8,128)S(1)} %fusion.71, ...), kind=kOutput, calls=%fused_computation.61 | convolution fusion | flops 409468800 | bytes 3851008 | tf_op jit(solution)/shard_map/hij,jhp->ihp/dot_general | solution.py:63
  114.6 1.4 copy.99
  116.0 2.2 fusion.46
  118.2 2.1 subtract_multiply_fusion
  120.3 1.6 fusion.49
  122.0 0.5 iota_compare_fusion.1
  122.5 1.8 convolution_bitcast_fusion.2
  124.3 10.8 %fusion.8 = (f32[64,128]{1,0:T(8,128)}, f32[64,128]{1,0:T(8,128)}, f32[128,128]{1,0:T(8,128)S(1)}) fusion(f32[128,128]{1,0:T(8,128)S(1)} %fusion.71, f32[64,128]{1,0:T(8,128)} %copy.93, pred[128,128]{1,0:T(8,128)(4,1)} %copy-done.13, f32[128,64,32]{0,2,1:T(8,128)S(1)} %subtract_multiply_fusion, f32[128,64]{0,1:T(8,128)S(1)} %get-tuple-element.348, ...), kind=kOutput, calls=%fused_computation.12 | convolution fusion | flops 411533312 | bytes 1851392 | tf_op jit(solution)/shard_map/ihp,jhp->hij/dot_general | solution.py:78
  135.2 0.8 fusion.37
  136.0 65.4 %all-gather.8.cloned.1.call-done = f32[256,32,128]{2,1,0:T(8,128)} async-done(((f32[64,32,128]{2,1,0:T(8,128)}), f32[256,32,128]{2,1,0:T(8,128)}) %all-gather.8.cloned.1.call-update) | async-done | bytes 4194320 | tf_op jit(solution)/shard_map/all_gather | solution.py:12
  201.4 6.1 %while.31 = (s32[]{:T(128)}, f32[64,32,128]{2,1,0:T(8,128)S(1)}, s32[]{:T(128)}, f32[4,64]{1,0:T(4,128)S(1)}, f32[4,64,32,128]{3,2,1,0:T(8,128)}, /*index=5*/s32[]{:T(128)}, s32[]{:T(128)}, s32[]{:T(128)}, s32[]{:T(128)}) while((s32[]{:T(128)}, f32[64,32,128]{2,1,0:T(8,128)S(1)}, s32[]{:T(128)}, f32[4,64]{1,0:T(4,128)S(1)}, ...), condition=%wide.region_8.9_spmd.clone, body=%wide.region_7.8_spmd.clone.sunk | while | flops 1048584 | bytes 3146663 | solution.py:25
  201.4 1.5 fusion.105
  202.9 1.5 fusion.105
  204.5 1.5 fusion.105
  206.0 1.5 fusion.105
  207.6 0.6 convolution_bitcast_fusion
  208.2 0.6 multiply_reduce_fusion.2
  208.8 1.9 convolution_bitcast_fusion.3
  210.7 4.9 %multiply_reduce_fusion.1 = (f32[64]{0:T(128)S(1)}, f32[128,64]{0,1:T(8,128)S(1)}, f32[128,64]{0,1:T(8,128)S(1)}, f32[128,64]{0,1:T(8,128)S(1)}, bf16[128,64,32]{0,2,1:T(8,128)(2,1)S(1)}) fusion(f32[128,64,32]{0,2,1:T(8,128)S(1)} %subtract_multiply_fusion, f32[128,64,32]{0,2,1:T(8,128)S(1)} %convolution_bitcast_fusion, ...), kind=kOutput, calls=%fused_computation.53 | convolution fusion | flops 409968576 | bytes 4473344 | tf_op jit(solution)/shard_map/hij,ihp->jhp/dot_general | solution.py:77
  215.6 0.1 multiply_reduce_fusion.8
  215.7 0.1 fusion.64
  215.8 0.1 rev.7
  215.9 0.1 copy.100
  216.0 0.2 reduce_window_sum.25
  216.2 0.1 copy.101
  216.2 0.1 rev.8
  216.3 0.9 fusion.38
  217.2 1.0 copy.102
  218.2 0.8 multiply_reduce_fusion.7
  219.0 7.2 %all-reduce = (f32[64]{0:T(128)S(1)}, f32[64]{0:T(128)S(1)}, f32[2048]{0:T(1024)S(1)}) all-reduce(f32[64]{0:T(128)S(1)} %get-tuple-element.344, f32[64]{0:T(128)S(1)} %get-tuple-element.311, f32[2048]{0:T(1024)S(1)} %get-tuple-element.309), channel_id=1, replica_groups=mesh['groups'=2,'seq'=4,'dp'=4] {'dp'}, use_global_device_ids=true, to_apply=%region_19.20 | all-reduce | flops 2176 | bytes 17408 | tf_op jit(solution)/shard_map/psum | solution.py:105
  226.2 10.0 %all-reduce.1 = (f32[64]{0:T(128)}, f32[64]{0:T(128)}, f32[2048]{0:T(1024)}) all-reduce(f32[64]{0:T(128)S(1)} %get-tuple-element.335, f32[64]{0:T(128)S(1)} %get-tuple-element.336, f32[2048]{0:T(1024)S(1)} %get-tuple-element.337), channel_id=1, replica_groups=mesh['groups'=2,'seq'=4,'dp'=4] {'seq'}, use_global_device_ids=true, to_apply=%region_20.21 | all-reduce | flops 2176 | bytes 17408 | tf_op jit(solution)/shard_map/psum | solution.py:104
  (55 shorter events, 0.2 us)
Async XLA Ops:
  7.2 7.1 %copy-start = (bf16[1,128,128]{2,1,0:T(8,128)(2,1)S(1)}, bf16[1,128,128]{2,1,0:T(8,128)(2,1)}, u32[]{:S(2)}) copy-start(bf16[1,128,128]{2,1,0:T(8,128)(2,1)} %param.16) | copy-start | bytes 98308
  7.2 10.7 %copy-start.4 = (bf16[1,128,2048]{2,1,0:T(8,128)(2,1)S(1)}, bf16[1,128,2048]{2,1,0:T(8,128)(2,1)}, u32[]{:S(2)}) copy-start(bf16[1,128,2048]{2,1,0:T(8,128)(2,1)} %param.23) | copy-start | bytes 1572868
  7.2 92.3 %all-gather.6.cloned.1.call-start = ((), (), s32[]{:S(2)}) async-start(), calls=%async_computation | async-start | bytes 5242880 | tf_op jit(solution)/shard_map/all_gather | solution.py:12
  14.0 85.5 %copy-start.2 = (bf16[1,128,2048]{1,2,0:T(8,128)(2,1)}, bf16[1,128,2048]{1,2,0:T(8,128)(2,1)S(1)}, u32[]{:S(2)}) copy-start(bf16[1,128,2048]{1,2,0:T(8,128)(2,1)S(1)} %copy.90) | copy-start | bytes 1572868
  14.0 5.1 %copy-start.9 = (f32[2048]{0:T(1024)S(1)}, f32[2048]{0:T(1024)}, u32[]{:S(2)}) copy-start(f32[2048]{0:T(1024)} %param.21) | copy-start | bytes 24580
  14.0 17.9 %copy-start.7 = (bf16[1,128,128]{2,1,0:T(8,128)(2,1)S(1)}, bf16[1,128,128]{2,1,0:T(8,128)(2,1)}, u32[]{:S(2)}) copy-start(bf16[1,128,128]{2,1,0:T(8,128)(2,1)} %param.17) | copy-start | bytes 98308
  15.9 185.5 %all-gather.8.cloned.1.call-start = ((), (), s32[]{:S(2)}) async-start(), calls=%async_computation.1 | async-start | bytes 5242880 | tf_op jit(solution)/shard_map/all_gather | solution.py:12
  31.9 74.3 %copy-start.13 = (pred[128,128]{1,0:T(8,128)(4,1)}, pred[128,128]{1,0:T(8,128)(4,1)S(1)}, u32[]{:S(2)}) copy-start(pred[128,128]{1,0:T(8,128)(4,1)S(1)} %fusion.62) | copy-start | bytes 49156
  99.5 6.7 %copy-start.17 = (f32[64]{0:T(128)S(1)}, f32[64]{0:T(128)}, u32[]{:S(2)}) copy-start(f32[64]{0:T(128)} %param.20) | copy-start | bytes 772
  106.2 8.4 %copy-start.5 = (f32[128,64,32]{0,2,1:T(8,128)}, f32[128,64,32]{0,2,1:T(8,128)S(1)}, u32[]{:S(2)}) copy-start(f32[128,64,32]{0,2,1:T(8,128)S(1)} %convolution_bitcast_fusion.1) | copy-start | bytes 3145732
  114.6 3.6 %copy-start.1 = (f32[128,64,32]{0,2,1:T(8,128)}, f32[128,64,32]{0,2,1:T(8,128)S(1)}, u32[]{:S(2)}) copy-start(f32[128,64,32]{0,2,1:T(8,128)S(1)} %get-tuple-element.355) | copy-start | bytes 3145732
  207.5 1.2 copy-start.3
  207.5 3.1 %copy-start.6 = (f32[128,64,32]{0,2,1:T(8,128)S(1)}, f32[128,64,32]{0,2,1:T(8,128)}, u32[]{:S(2)}) copy-start(f32[128,64,32]{0,2,1:T(8,128)} %copy-done.5) | copy-start | bytes 3145732
  207.5 3.1 %copy-start.10 = (f32[64,128]{1,0:T(8,128)S(1)}, f32[64,128]{1,0:T(8,128)}, u32[]{:S(2)}) copy-start(f32[64,128]{1,0:T(8,128)} %copy.93) | copy-start | bytes 98308
  207.6 3.1 %copy-start.14 = (pred[128,128]{1,0:T(8,128)(4,1)S(1)}, pred[128,128]{1,0:T(8,128)(4,1)}, u32[]{:S(2)}) copy-start(pred[128,128]{1,0:T(8,128)(4,1)} %copy-done.13) | copy-start | bytes 49156
  207.6 3.1 %copy-start.18 = (f32[64]{0:T(128)S(1)}, f32[64]{0:T(128)}, u32[]{:S(2)}) copy-start(f32[64]{0:T(128)} %param.20) | copy-start | bytes 772
  210.7 5.0 %copy-start.11 = (f32[64,128]{1,0:T(8,128)S(1)}, f32[64,128]{1,0:T(8,128)}, u32[]{:S(2)}) copy-start(f32[64,128]{1,0:T(8,128)} %get-tuple-element.306) | copy-start | bytes 98308
  210.7 5.0 %copy-start.12 = (f32[64,128]{1,0:T(8,128)S(1)}, f32[64,128]{1,0:T(8,128)}, u32[]{:S(2)}) copy-start(f32[64,128]{1,0:T(8,128)} %get-tuple-element.307) | copy-start | bytes 98308
  210.7 5.0 %copy-start.16 = (pred[128]{0:T(512)(128)(4,1)S(1)}, pred[128]{0:T(512)(128)(4,1)}, u32[]{:S(2)}) copy-start(pred[128]{0:T(512)(128)(4,1)} %iota_compare_fusion.1) | copy-start | bytes 388
  210.7 7.5 %copy-start.8 = (f32[1,128,64]{1,2,0:T(8,128)S(1)}, f32[1,128,64]{1,2,0:T(8,128)}, u32[]{:S(2)}) copy-start(f32[1,128,64]{1,2,0:T(8,128)} %param.18) | copy-start | bytes 98308
  210.7 7.5 %copy-start.15 = (f32[64]{0:T(128)S(1)}, f32[64]{0:T(128)}, u32[]{:S(2)}) copy-start(f32[64]{0:T(128)} %get-tuple-element.350) | copy-start | bytes 772
Sparse Core Ops, SparseCore 0:
  16.0 83.4 all-gather.5
  122.1 79.2 all-gather.7
